TPU v7x, 512 devices: a whole 4x8x8 slice. The times are simulated.
512 devices in a mesh: req: 32 (over x, z), tp: 16 (over y, core).
Axes of the slice: x: 4, y: 8, z: 8, core: 2. Of those that a mesh axis runs over, the one named last changes fastest.
Arguments:
- hidden: bfloat16 [32768, 2048], P(('req', 'tp')), may hold values from -6 to 6
- ln_gain: float32 [2048], replicated, may hold values from 0.1 to 1.9
- w_qkv: bfloat16 [2048, 3, 2048], P(None, None, 'tp'), may hold values from -0.125 to 0.125
- w_out: bfloat16 [2048, 2048], P('tp'), may hold values from -0.125 to 0.125
- cache_kv: bfloat16 [2, 512, 256, 2048], P(None, 'req', None, 'tp'), may hold values from -6 to 6
- cache_len: int32 [512], P('req'), may hold values from 16 to 256, as said below
- ancestors: int32 [512, 64, 64], P('req'), may hold values from 0 to 1, as said below
- accepted: int32 [512, 8], P('req'), may hold values from 0 to 14, as said below
Outputs:
- attn_proj: bfloat16 [32768, 2048], P(('req', 'tp'))
- kept_kv: bfloat16 [2, 512, 8, 2048], P(None, 'req', None, 'tp')
Inputs may be any that keep to these rules, and one draw needn't show every extreme that they name: `cache_len`: at least one request of the whole batch has exactly 256 cached positions. `ancestors`: entry (r, i, j) is 1 exactly where draft token j is token i or an ancestor of it in request r's tree; a token's parent has a lower index and token 0 is the root. `accepted`: each row holds, in increasing order, the first 8 tokens of a path down from the root of the request's tree, each entry the parent of the next.
All inputs are finite; a program needn't handle non-finite values.
Results may differ from a plain program's by a relative error of at most 0.018.
Values may be sent and summed in bfloat16 or wider, within the bound.
A program may use at most 64 MiB of HBM per device.

v0:
```python
import math
import jax
import jax.numpy as jnp
from jax import lax
from jax.sharding import PartitionSpec as P

HD = 128
KEY_BLOCK = 128


def block_part(queries, keys, values, positions, valid, slopes):
    heads = queries.shape[2]
    keys_four = keys.reshape(keys.shape[0], keys.shape[1], heads, HD)
    values_four = values.reshape(values.shape[0], values.shape[1], heads, HD)
    scores = jnp.einsum(
        "rihd,rjhd->rhij", queries, keys_four, preferred_element_type=jnp.float32
    ) * (1.0 / math.sqrt(HD))
    scores = scores + slopes[None, :, None, None] * positions[:, None, None, :]
    allowed = valid[:, None, :, :]
    scores = jnp.where(allowed, scores, -1e30)
    top = jnp.max(scores, axis=3)
    expo = jnp.where(allowed, jnp.exp(scores - top[..., None]), 0.0)
    total = jnp.sum(expo, axis=3)
    weights = expo.astype(jnp.bfloat16)
    summed = jnp.einsum("rhij,rjhd->rihd", weights, values_four, preferred_element_type=jnp.float32)
    return (top, total, summed)


def combine(first, second):
    top = jnp.maximum(first[0], second[0])
    scale_one = jnp.exp(first[0] - top)
    scale_two = jnp.exp(second[0] - top)
    total = first[1] * scale_one + second[1] * scale_two
    summed = (
        first[2] * jnp.transpose(scale_one, (0, 2, 1))[..., None]
        + second[2] * jnp.transpose(scale_two, (0, 2, 1))[..., None]
    )
    return (top, total, summed)


def cache_sweep(queries, keys, values, lengths, stride, slopes):
    requests, drafts, heads = (queries.shape[0], queries.shape[1], queries.shape[2])
    start_state = (
        jnp.full((requests, heads, drafts), -1e30, jnp.float32),
        jnp.zeros((requests, heads, drafts), jnp.float32),
        jnp.zeros((requests, drafts, heads, HD), jnp.float32),
    )
    count = keys.shape[1] // KEY_BLOCK

    def advance(block_index, state):
        start = block_index * KEY_BLOCK
        key_block = lax.dynamic_slice_in_dim(keys, start, KEY_BLOCK, 1)
        value_block = lax.dynamic_slice_in_dim(values, start, KEY_BLOCK, 1)
        cells = (start + jnp.arange(KEY_BLOCK)) * stride
        valid = (cells[None, :] < lengths[:, None])[:, None, :]
        positions = jnp.broadcast_to(cells.astype(jnp.float32)[None, :], (requests, KEY_BLOCK))
        return combine(state, block_part(queries, key_block, value_block, positions, valid, slopes))

    return lax.fori_loop(0, count, advance, start_state)


def on_device(hidden, ln_gain, w_qkv, w_out, cache_kv, cache_len, ancestors, accepted):
    values_f = hidden.astype(jnp.float32)
    mean = jnp.mean(values_f, axis=1, keepdims=True)
    centered = values_f - mean
    var = jnp.mean(centered * centered, axis=1, keepdims=True)
    normed = (centered * lax.rsqrt(var + 1e-05) * ln_gain[None, :]).astype(jnp.bfloat16)
    width = w_qkv.shape[2]
    heads = width // HD
    flat_weight = w_qkv.reshape(w_qkv.shape[0], 3 * width)
    joined = jnp.dot(
        lax.all_gather(normed, "tp", axis=0, tiled=True),
        flat_weight,
        preferred_element_type=jnp.float32,
    )
    requests = cache_len.shape[0]
    drafts = ancestors.shape[1]
    joined = joined.astype(jnp.bfloat16).reshape(requests, drafts, 3, heads, HD)
    queries = joined[:, :, 0]
    new_keys = joined[:, :, 1].reshape(requests, drafts, width)
    new_values = joined[:, :, 2].reshape(requests, drafts, width)
    head_ids = lax.axis_index("tp") * heads + jnp.arange(heads)
    all_heads = heads * lax.axis_size("tp")
    slopes = jnp.exp2(-8.0 * (head_ids.astype(jnp.float32) + 1.0) / all_heads)
    depth = jnp.sum(ancestors, axis=2) - 1
    draft_pos = (cache_len[:, None] + depth).astype(jnp.float32)
    draft_part = block_part(queries, new_keys, new_values, draft_pos, ancestors == 1, slopes)
    cache_part = cache_sweep(queries, cache_kv[0], cache_kv[1], cache_len, 1, slopes)
    merged = combine(cache_part, draft_part)
    attn = (merged[2] / jnp.transpose(merged[1], (0, 2, 1))[..., None]).astype(jnp.bfloat16)
    attn = attn.reshape(requests * drafts, width)
    attn_proj = lax.psum_scatter(
        jnp.dot(attn, w_out, preferred_element_type=jnp.float32).astype(jnp.bfloat16),
        "tp",
        scatter_dimension=0,
        tiled=True,
    )
    onehot = (accepted[:, :, None] == jnp.arange(drafts)[None, None, :]).astype(jnp.bfloat16)
    kept_keys = jnp.einsum("rad,rdc->rac", onehot, new_keys, preferred_element_type=jnp.float32)
    kept_values = jnp.einsum("rad,rdc->rac", onehot, new_values, preferred_element_type=jnp.float32)
    kept_kv = jnp.stack([kept_keys, kept_values]).astype(jnp.bfloat16)
    return (attn_proj, kept_kv)


def solution(mesh):
    placed = (
        P(("req", "tp"), None),
        P(),
        P(None, None, "tp"),
        P("tp", None),
        P(None, "req", None, "tp"),
        P("req"),
        P("req", None, None),
        P("req", None),
    )
    return jax.shard_map(
        on_device,
        mesh=mesh,
        in_specs=placed,
        out_specs=(P(("req", "tp"), None), P(None, "req", None, "tp")),
        check_vma=False,
    )
```

profile of v0, /device:TPU:2, one launch (start us, length us, event | category | flops | bytes accessed | tf_op | source)
XLA Modules:
  0.0 154.7 jit_solution(12655179019747754380)
XLA Ops:
  7.2 1.2 convert_reduce_fusion
  8.4 1.2 fusion.33
  9.6 1.8 %fusion.35 = bf16[64,2048]{1,0:T(8,128)(2,1)} fusion(bf16[64,2048]{1,0:T(8,128)(2,1)} %param.10, f32[2048]{0:T(1024)} %param.11, f32[64]{0:T(128)S(1)} %add_rsqrt_fusion, f32[64]{0:T(128)S(1)} %broadcast_multiply_fusion), kind=kLoop, calls=%fused_computation.56 | loop fusion | flops 655360 | bytes 532992 | tf_op jit(solution)/shard_map/convert_element_type | solution.py:67
  11.6 1.2 copy.18
  13.2 2.6 %copy.16 = bf16[2048,3,128]{0,2,1:T(8,128)(2,1)} copy(bf16[2048,3,128]{2,0,1:T(8,128)(2,1)} %param.12) | data formatting | bytes 3145728 | tf_op args[2]
  15.9 0.7 broadcast_compare_fusion.1
  16.7 2.7 %slice_bitcast_fusion = (bf16[16,256,128]{2,1,0:T(8,128)(2,1)S(1)}, bf16[16,256,128]{2,1,0:T(8,128)(2,1)}) fusion(bf16[2,16,256,128]{3,2,1,0:T(8,128)(2,1)} %param.14), kind=kLoop, calls=%fused_computation.48 | loop fusion | bytes 4194304 | tf_op jit(solution)/shard_map/squeeze | solution.py:88
  19.4 41.4 %all-gather.2.cloned.1.call-done = bf16[1024,2048]{1,0:T(8,128)(2,1)} async-done(((bf16[64,2048]{1,0:T(8,128)(2,1)}), bf16[1024,2048]{1,0:T(8,128)(2,1)}) %all-gather.2.cloned.1.call-update) | async-done | bytes 4194320 | tf_op jit(solution)/shard_map/all_gather | solution.py:72
  60.8 5.9 %convolution_convert_fusion.1 = bf16[1024,384]{1,0:T(8,128)(2,1)} fusion(bf16[1024,2048]{1,0:T(8,128)(2,1)} %all-gather.2.cloned.1.call-done, bf16[2048,384]{0,1:T(8,128)(2,1)} %bitcast.129), kind=kOutput, calls=%fused_computation.34 | convolution fusion | flops 1611005952 | bytes 6553600 | tf_op jit(solution)/shard_map/dot_general | solution.py:71
  66.7 2.4 %reshape.195 = bf16[16,64,3,1,128]{4,2,1,0,3:T(4,128)(2,1)S(1)} reshape(bf16[1024,384]{1,0:T(8,128)(2,1)} %convolution_convert_fusion.1) | data formatting | bytes 1572864 | tf_op jit(solution)/shard_map/reshape | solution.py:78
  69.2 2.2 %fusion.53 = (bf16[16,64,1,1,128]{4,2,1,0,3:T(2,128)(2,1)}, bf16[16,64,1,1,128]{4,2,1,0,3:T(2,128)(2,1)}, bf16[16,64,1,1,128]{4,2,1,0,3:T(2,128)(2,1)S(1)}) fusion(bf16[16,64,3,1,128]{4,2,1,0,3:T(4,128)(2,1)S(1)} %reshape.195), kind=kLoop, calls=%fused_computation.86 | loop fusion | bytes 1572864 | tf_op jit(solution)/shard_map/slice | solution.py:81
  71.4 0.8 copy-done.4
  72.2 5.6 %while.18 = (s32[]{:T(128)}, f32[16,1,64]{2,0,1:T(8,128)S(1)}, f32[16,1,64]{2,0,1:T(8,128)S(1)}, f32[16,64,1,128]{3,1,0,2:T(8,128)S(1)}, s32[16]{0:T(128)S(1)}, ...) while((s32[]{:T(128)}, f32[16,1,64]{2,0,1:T(8,128)S(1)}, ...), condition=%wide.region_5.6_spmd.clone, body=%wide.region_2.5_spmd.clone.sunk | while | flops 68954632 | bytes 4032779 | solution.py:59
  72.3 1.6 %fusion.68 = (f32[16,64]{1,0:T(8,128)S(1)}, f32[16,64,128]{2,1,0:T(8,128)S(1)}) fusion(f32[128]{0:T(128)S(1)} %convert_multiply_fusion.3, bf16[16,64,1,128]{3,1,0,2:T(8,128)(2,1)S(1)} %get-tuple-element.324, bf16[16,256,128]{2,1,0:T(8,128)(2,1)} %get-tuple-element.323, s32[]{:T(128)S(6)} %select_n.64, pred[16,128]{1,0:T(8,128)(4,1)S(1)} %broadcast_compare_fusion.3), kind=kOutput, calls=%fused_computation.85.clone.1 | convolution fusion | flops 34077696 | bytes 1317380 | tf_op jit(solution)/shard_map/while/body/eval_jaxpr/rihd,rjhd->rhij/dot_general | solution.py:15
  73.9 0.4 fusion.70
  74.4 0.6 fusion.72
  75.1 1.6 %fusion.68 = (f32[16,64]{1,0:T(8,128)S(1)}, f32[16,64,128]{2,1,0:T(8,128)S(1)}) fusion(f32[128]{0:T(128)S(1)} %convert_multiply_fusion.3, bf16[16,64,1,128]{3,1,0,2:T(8,128)(2,1)S(1)} %get-tuple-element.324, bf16[16,256,128]{2,1,0:T(8,128)(2,1)} %get-tuple-element.323, s32[]{:T(128)S(6)} %select_n.64, pred[16,128]{1,0:T(8,128)(4,1)S(1)} %broadcast_compare_fusion.3), kind=kOutput, calls=%fused_computation.85.clone.1 | convolution fusion | flops 34077696 | bytes 1317380 | tf_op jit(solution)/shard_map/while/body/eval_jaxpr/rihd,rjhd->rhij/dot_general | solution.py:15
  77.1 0.6 fusion.72
  77.8 1.6 %fusion.54 = (f32[16,64]{1,0:T(8,128)S(1)}, f32[16,64,64]{1,2,0:T(8,128)S(1)}) fusion(pred[16,64,64]{1,2,0:T(32,128)(4,1)} %broadcast_compare_fusion.1, f32[16,64]{1,0:T(8,128)S(1)} %convert_multiply_fusion.1, bf16[16,64,1,1,128]{4,2,1,0,3:T(2,128)(2,1)} %get-tuple-element.218, bf16[16,64,1,1,128]{4,2,1,0,3:T(2,128)(2,1)} %copy-done.4), kind=kOutput, calls=%fused_computation.87 | convolution fusion | flops 17038336 | bytes 860160 | tf_op jit(solution)/shard_map/rihd,rjhd->rhij/dot_general | solution.py:15
  79.6 0.6 fusion.28
  80.2 3.2 %convolution_convert_fusion = bf16[1024,2048]{1,0:T(8,128)(2,1)} fusion(bf16[1024,128]{1,0:T(8,128)(2,1)S(1)} %bitcast.130, bf16[128,2048]{1,0:T(8,128)(2,1)S(1)} %copy-done), kind=kOutput, calls=%fused_computation.33 | convolution fusion | flops 538968064 | bytes 4980736 | tf_op jit(solution)/shard_map/dot_general | solution.py:93
  83.4 0.7 copy-done.9
  84.9 0.6 pad_maximum_fusion
  85.6 62.3 %reduce-scatter.2.cloned.1.call-done = bf16[64,2048]{1,0:T(8,128)(2,1)} async-done(((bf16[1024,2048]{1,0:T(8,128)(2,1)}), bf16[64,2048]{1,0:T(8,128)(2,1)}) %reduce-scatter.2.cloned.1.call-update) | async-done | bytes 262160 | tf_op jit(solution)/shard_map/reduce_scatter | solution.py:92
  (48 shorter events, 2.3 us)
Async XLA Ops:
  7.2 73.0 %copy-start = (bf16[128,2048]{1,0:T(8,128)(2,1)S(1)}, bf16[128,2048]{1,0:T(8,128)(2,1)}, u32[]{:S(2)}) copy-start(bf16[128,2048]{1,0:T(8,128)(2,1)} %param.13) | copy-start | bytes 1572868
  7.2 5.6 %copy-start.3 = (s32[16,64,64]{2,1,0:T(8,128)S(1)}, s32[16,64,64]{2,1,0:T(8,128)}, u32[]{:S(2)}) copy-start(s32[16,64,64]{2,1,0:T(8,128)} %param.16) | copy-start | bytes 786436
  7.2 53.6 %all-gather.2.cloned.1.call-start = ((), (), s32[]{:S(2)}) async-start(), calls=%async_computation.1 | async-start | bytes 4456448 | tf_op jit(solution)/shard_map/all_gather | solution.py:72
  11.5 136.4 %reduce-scatter.2.cloned.1.call-start = ((), (), s32[]{:S(2)}) async-start(), calls=%async_computation.2 | async-start | bytes 4456448 | tf_op jit(solution)/shard_map/reduce_scatter | solution.py:92
  12.8 3.1 %copy-start.1 = (s32[16,64,64]{1,2,0:T(8,128)}, s32[16,64,64]{1,2,0:T(8,128)S(1)}, u32[]{:S(2)}) copy-start(s32[16,64,64]{1,2,0:T(8,128)S(1)} %copy.18) | copy-start | bytes 786436
  12.8 3.0 %copy-start.8 = (s32[16]{0:T(128)S(1)}, s32[16]{0:T(128)}, u32[]{:S(2)}) copy-start(s32[16]{0:T(128)} %param.15) | copy-start | bytes 196
  71.4 0.8 copy-start.4
  72.2 7.2 %copy-start.2 = (s32[16,64,64]{1,2,0:T(8,128)S(1)}, s32[16,64,64]{1,2,0:T(8,128)}, u32[]{:S(2)}) copy-start(s32[16,64,64]{1,2,0:T(8,128)} %copy-done.1) | copy-start | bytes 786436
  77.8 1.8 %copy-start.5 = (bf16[16,64,1,1,128]{4,2,1,0,3:T(2,128)(2,1)S(1)}, bf16[16,64,1,1,128]{4,2,1,0,3:T(2,128)(2,1)}, u32[]{:S(2)}) copy-start(bf16[16,64,1,1,128]{4,2,1,0,3:T(2,128)(2,1)} %get-tuple-element.217) | copy-start | bytes 786436
  77.8 1.8 %copy-start.7 = (pred[16,64,64]{1,2,0:T(32,128)(4,1)S(1)}, pred[16,64,64]{1,2,0:T(32,128)(4,1)}, u32[]{:S(2)}) copy-start(pred[16,64,64]{1,2,0:T(32,128)(4,1)} %broadcast_compare_fusion.1) | copy-start | bytes 196612
  83.4 0.7 copy-start.9
  83.4 1.1 copy-start.6
Sparse Core Ops, SparseCore 0:
  11.6 49.1 all-gather.1
  83.5 64.3 reduce-scatter.1
where the time goes:
time: 155 us
  waiting for transfers between devices  104 us (67%)
  matrix products  16.2 us (10%)
  between operations  14.3 us (9%)
  local copies, waits for them, and re-layouts  13.1 us (8%)
  other arithmetic  7.15 us (5%)
    reduce_scatter x1, waiting for transfers between devices, on_device(): lax.psum_scatter(jnp.dot(attn, w_out, preferred_element_type=jnp.float32)...  62.3 us
    all_gather x1, waiting for transfers between devices, on_device(): lax.all_gather(normed, 'tp', axis=0, tiled=True)  41.4 us
    dot_general x1, matrix products, on_device(): jnp.dot(lax.all_gather(normed, 'tp', axis=0, tiled=True), flat_weight, pr...  5.92 us
    unnamed x24, local copies, waits for them, and re-layouts  5.73 us
    dot_general x3, matrix products, block_part(): jnp.einsum('rihd,rjhd->rhij', queries, keys_four, preferred_element_type=...  4.81 us
    dot_general x1, matrix products, on_device(): jnp.dot(attn, w_out, preferred_element_type=jnp.float32)  3.18 us
  transfers between devices with their start and end apart: 2, of which 2 were waited for; matrix products, arithmetic and copies ran while one was open for 6% of the time, Pallas kernels for 0%

commit v1 on v0

--- a/solution.py
+++ b/solution.py
@@ -69,7 +69,9 @@
     heads = width // HD
     flat_weight = w_qkv.reshape(w_qkv.shape[0], 3 * width)
     joined = jnp.dot(
-        lax.all_gather(normed, "tp", axis=0, tiled=True),
+        jnp.concatenate(
+            lax.all_to_all(jnp.stack([normed] * lax.axis_size("tp")), "tp", 0, 0), axis=0
+        ),
         flat_weight,
         preferred_element_type=jnp.float32,
     )

time: 155 us -> 213 us (1.37)
  the two profiles are of different devices: /device:TPU:2 before, /device:TPU:27 now
where the time goes in v1:
time: 213 us
  waiting for transfers between devices  153 us (72%)
  matrix products  17.2 us (8%)
  local copies, waits for them, and re-layouts  14.3 us (7%)
  between operations  14.3 us (7%)
  starting transfers between devices  7.82 us (4%)
  other arithmetic  6.42 us (3%)
    all_to_all x1, waiting for transfers between devices, on_device(): lax.all_to_all(jnp.stack([normed] * lax.axis_size('tp')), 'tp', 0, 0)  86.8 us
    reduce_scatter x1, waiting for transfers between devices, on_device(): lax.psum_scatter(jnp.dot(attn, w_out, preferred_element_type=jnp.float32)...  65.8 us
    all_to_all x1, starting transfers between devices, on_device(): lax.all_to_all(jnp.stack([normed] * lax.axis_size('tp')), 'tp', 0, 0)  7.78 us
    dot_general x1, matrix products, on_device(): jnp.dot(jnp.concatenate(lax.all_to_all(jnp.stack([normed] * lax.axis_size...  5.91 us
    dot_general x3, matrix products, block_part(): jnp.einsum('rihd,rjhd->rhij', queries, keys_four, preferred_element_type=...  4.75 us
    unnamed x22, local copies, waits for them, and re-layouts  4.43 us
  transfers between devices with their start and end apart: 2, of which 2 were waited for; matrix products, arithmetic and copies ran while one was open for 4% of the time, Pallas kernels for 0%

profile of v1, /device:TPU:27, one launch (start us, length us, event | category | flops | bytes accessed | tf_op | source)
XLA Modules:
  0.0 212.7 jit_solution(16530677186553712430)
XLA Ops:
  7.2 1.1 convert_reduce_fusion
  8.3 1.2 fusion.33
  9.5 1.1 fusion.35
  10.7 2.5 %stack.11 = bf16[16,64,2048]{2,1,0:T(8,128)(2,1)} broadcast(bf16[64,2048]{1,0:T(8,128)(2,1)S(1)} %fusion.35), dimensions={1,2} | broadcast | bytes 4456448 | tf_op jit(solution)/shard_map/stack | solution.py:73
  13.2 7.8 %all-to-all-start = ((bf16[16,64,2048]{2,1,0:T(8,128)(2,1)}), bf16[16,64,2048]{2,1,0:T(8,128)(2,1)}, u32[]{:S(2)}, u32[]{:S(2)}) async-start(bf16[16,64,2048]{2,1,0:T(8,128)(2,1)} %stack.11), calls=%async_computation | async-start | bytes 8388608 | tf_op jit(solution)/shard_map/all_to_all | solution.py:73
  21.6 2.7 %copy.16 = bf16[2048,3,128]{0,2,1:T(8,128)(2,1)} copy(bf16[2048,3,128]{2,0,1:T(8,128)(2,1)} %param.12) | data formatting | bytes 3145728 | tf_op args[2]
  24.4 0.7 broadcast_compare_fusion.1
  25.1 2.7 %slice_bitcast_fusion = (bf16[16,256,128]{2,1,0:T(8,128)(2,1)S(1)}, bf16[16,256,128]{2,1,0:T(8,128)(2,1)}) fusion(bf16[2,16,256,128]{3,2,1,0:T(8,128)(2,1)} %param.14), kind=kLoop, calls=%fused_computation.48 | loop fusion | bytes 4194304 | tf_op jit(solution)/shard_map/squeeze | solution.py:90
  27.9 86.8 %all-to-all-done = bf16[16,64,2048]{2,1,0:T(8,128)(2,1)} async-done(((bf16[16,64,2048]{2,1,0:T(8,128)(2,1)}), bf16[16,64,2048]{2,1,0:T(8,128)(2,1)}, u32[]{:S(2)}, u32[]{:S(2)}) %all-to-all-start) | async-done | bytes 4194336 | tf_op jit(solution)/shard_map/all_to_all | solution.py:73
  114.7 5.9 %convolution_convert_fusion.1 = bf16[1024,384]{1,0:T(8,128)(2,1)} fusion(bf16[1024,2048]{1,0:T(8,128)(2,1)} %bitcast.1, bf16[2048,384]{0,1:T(8,128)(2,1)} %bitcast.130), kind=kOutput, calls=%fused_computation.34 | convolution fusion | flops 1611005952 | bytes 6553600 | tf_op jit(solution)/shard_map/dot_general | solution.py:71
  120.6 2.4 %reshape.201 = bf16[16,64,3,1,128]{4,2,1,0,3:T(4,128)(2,1)S(1)} reshape(bf16[1024,384]{1,0:T(8,128)(2,1)} %convolution_convert_fusion.1) | data formatting | bytes 1572864 | tf_op jit(solution)/shard_map/reshape | solution.py:80
  123.0 2.2 %fusion.53 = (bf16[16,64,1,1,128]{4,2,1,0,3:T(2,128)(2,1)}, bf16[16,64,1,1,128]{4,2,1,0,3:T(2,128)(2,1)}, bf16[16,64,1,1,128]{4,2,1,0,3:T(2,128)(2,1)S(1)}) fusion(bf16[16,64,3,1,128]{4,2,1,0,3:T(4,128)(2,1)S(1)} %reshape.201), kind=kLoop, calls=%fused_computation.86 | loop fusion | bytes 1572864 | tf_op jit(solution)/shard_map/slice | solution.py:83
  125.2 0.7 copy-done.4
  126.0 5.6 %while.18 = (s32[]{:T(128)}, f32[16,1,64]{2,0,1:T(8,128)S(1)}, f32[16,1,64]{2,0,1:T(8,128)S(1)}, f32[16,64,1,128]{3,1,0,2:T(8,128)S(1)}, s32[16]{0:T(128)S(1)}, ...) while((s32[]{:T(128)}, f32[16,1,64]{2,0,1:T(8,128)S(1)}, ...), condition=%wide.region_5.6_spmd.clone, body=%wide.region_2.5_spmd.clone.sunk | while | flops 68954632 | bytes 4032779 | solution.py:59
  126.1 1.6 fusion.68
  128.2 0.6 fusion.72
  128.9 1.6 fusion.68
  130.9 0.6 fusion.72
  131.6 1.5 fusion.54
  133.3 1.7 fusion.28
  135.0 3.2 %convolution_convert_fusion = bf16[1024,2048]{1,0:T(8,128)(2,1)} fusion(bf16[1024,128]{1,0:T(8,128)(2,1)S(1)} %bitcast.131, bf16[128,2048]{1,0:T(8,128)(2,1)S(1)} %copy-done), kind=kOutput, calls=%fused_computation.33 | convolution fusion | flops 538968064 | bytes 4980736 | tf_op jit(solution)/shard_map/dot_general | solution.py:95
  138.5 0.7 copy-done.5
  139.4 0.6 pad_maximum_fusion
  140.1 65.8 %reduce-scatter.2.cloned.1.call-done = bf16[64,2048]{1,0:T(8,128)(2,1)} async-done(((bf16[1024,2048]{1,0:T(8,128)(2,1)}), bf16[64,2048]{1,0:T(8,128)(2,1)}) %reduce-scatter.2.cloned.1.call-update) | async-done | bytes 262160 | tf_op jit(solution)/shard_map/reduce_scatter | solution.py:94
  (46 shorter events, 2.5 us)
Async XLA Ops:
  7.2 127.8 %copy-start = (bf16[128,2048]{1,0:T(8,128)(2,1)S(1)}, bf16[128,2048]{1,0:T(8,128)(2,1)}, u32[]{:S(2)}) copy-start(bf16[128,2048]{1,0:T(8,128)(2,1)} %param.13) | copy-start | bytes 1572868
  13.2 7.9 %copy-start.3 = (s32[16,64,64]{2,1,0:T(8,128)S(1)}, s32[16,64,64]{2,1,0:T(8,128)}, u32[]{:S(2)}) copy-start(s32[16,64,64]{2,1,0:T(8,128)} %param.16) | copy-start | bytes 786436
  13.2 101.5 %all-to-all-start = ((bf16[16,64,2048]{2,1,0:T(8,128)(2,1)}), bf16[16,64,2048]{2,1,0:T(8,128)(2,1)}, u32[]{:S(2)}, u32[]{:S(2)}) async-start(bf16[16,64,2048]{2,1,0:T(8,128)(2,1)} %stack.11), calls=%async_computation | async-start | bytes 8388608 | tf_op jit(solution)/shard_map/all_to_all | solution.py:73
  20.9 3.4 %copy-start.7 = (s32[16]{0:T(128)S(1)}, s32[16]{0:T(128)}, u32[]{:S(2)}) copy-start(s32[16]{0:T(128)} %param.15) | copy-start | bytes 196
  20.9 184.9 %reduce-scatter.2.cloned.1.call-start = ((), (), s32[]{:S(2)}) async-start(), calls=%async_computation.2 | async-start | bytes 4456448 | tf_op jit(solution)/shard_map/reduce_scatter | solution.py:94
  21.2 3.1 %copy-start.1 = (s32[16,64,64]{1,2,0:T(8,128)}, s32[16,64,64]{1,2,0:T(8,128)S(1)}, u32[]{:S(2)}) copy-start(s32[16,64,64]{1,2,0:T(8,128)S(1)} %copy.18) | copy-start | bytes 786436
  125.2 0.8 copy-start.4
  126.0 7.1 %copy-start.2 = (s32[16,64,64]{1,2,0:T(8,128)S(1)}, s32[16,64,64]{1,2,0:T(8,128)}, u32[]{:S(2)}) copy-start(s32[16,64,64]{1,2,0:T(8,128)} %copy-done.1) | copy-start | bytes 786436
  135.0 3.2 %copy-start.8 = (s32[16,8]{0,1:T(8,128)S(1)}, s32[16,8]{0,1:T(8,128)}, u32[]{:S(2)}) copy-start(s32[16,8]{0,1:T(8,128)} %param.17) | copy-start | bytes 1540
  135.0 3.3 %copy-start.6 = (bf16[16,64,1,1,128]{4,2,1,0,3:T(2,128)(2,1)S(1)}, bf16[16,64,1,1,128]{4,2,1,0,3:T(2,128)(2,1)}, u32[]{:S(2)}) copy-start(bf16[16,64,1,1,128]{4,2,1,0,3:T(2,128)(2,1)} %get-tuple-element.218) | copy-start | bytes 786436
  138.1 1.0 copy-start.5
Sparse Core Ops, SparseCore 0:
  138.3 67.5 reduce-scatter.1
